TPU v7x, 256 devices: a whole 4x4x8 slice. The times are simulated.
256 devices in a mesh: seq: 32 (over x, z), head: 8 (over y, core).
Axes of the slice: x: 4, y: 4, z: 8, core: 2. Of those that a mesh axis runs over, the one named last changes fastest.
Arguments:
- tokens: bfloat16 [16384, 4096], P('seq'), may hold values from -6 to 6
- w_xz: bfloat16 [4096, 2, 4096], P('seq', None, 'head'), may hold values from -0.09375 to 0.09375
- w_bc: bfloat16 [4096, 256], P('seq'), may hold values from -0.09375 to 0.09375
- conv_x: float32 [4, 4096], P(None, 'head'), may hold values from -3 to 3
- conv_bc: float32 [4, 256], replicated, may hold values from -3 to 3
- tail_x: bfloat16 [3, 4096], P(None, 'head'), may hold values from -6 to 6
- tail_bc: bfloat16 [3, 256], replicated, may hold values from -6 to 6
- decay_code: int32 [16384, 64], P('seq', 'head'), may hold values from 0 to 196608, as said below
- skip_gain: float32 [64], P('head'), may hold values from 0.5 to 2
- state_in: float32 [64, 64, 128], P('head'), may hold values from -180 to 180
- norm_gain: float32 [4096], P('head'), may hold values from 0.1 to 1.9
- w_out: bfloat16 [4096, 4096], P('head', 'seq'), may hold values from -0.1875 to 0.1875
Outputs:
- mixed: bfloat16 [16384, 4096], P('seq', 'head')
Inputs may be any that keep to these rules, and one draw needn't show every extreme that they name: `decay_code`: the decay factor of a token and head is exp(-code / 262144).
All inputs are finite; a program needn't handle non-finite values.
Results may differ from a plain program's by a relative error of at most 0.0085.
Values may be sent and summed in bfloat16 or wider, within the bound.
A program may use at most 128 MiB of HBM per device.

v0:
```python
import jax
import jax.numpy as jnp
from jax import lax
from jax.sharding import PartitionSpec as P

Q = 256


def passed_along(value, axis, by):
    size = lax.axis_size(axis)
    pairs = [(i, i + by) for i in range(size) if 0 <= i + by < size]
    return lax.ppermute(value, axis, pairs)


def depthwise(pre, tail, kernel):
    whole = jnp.concatenate([tail, pre], axis=0).astype(jnp.float32)
    length = pre.shape[0]
    total = jnp.zeros((length, pre.shape[1]), jnp.float32)
    for offset in range(kernel.shape[0]):
        total = total + kernel[offset] * whole[offset : offset + length]
    return jax.nn.silu(total).astype(jnp.bfloat16)


def entering_state(decay, end_state, state_in):
    count = lax.axis_size("seq")
    me = lax.axis_index("seq")
    first = me == 0
    lanes = end_state.shape[2]

    def pack(a, s):
        return jnp.concatenate(
            [s, jnp.broadcast_to(a[:, None, None], (a.shape[0], 1, lanes))], axis=1
        )

    got = passed_along(pack(decay, end_state), "seq", 1)
    acc_a = jnp.where(first, jnp.zeros_like(decay), got[:, -1, 0])
    acc_s = jnp.where(first, state_in, got[:, :-1])
    step = 1
    while step < count:
        far = passed_along(pack(acc_a, acc_s), "seq", step)
        has = me >= step
        acc_s = jnp.where(has, acc_a[:, None, None] * far[:, :-1] + acc_s, acc_s)
        acc_a = jnp.where(has, acc_a * far[:, -1, 0], acc_a)
        step *= 2
    return acc_s


def local(
    tokens,
    w_xz,
    w_bc,
    conv_x,
    conv_bc,
    tail_x,
    tail_bc,
    decay_code,
    skip_gain,
    state_in,
    norm_gain,
    w_out,
):
    rows = tokens.shape[0]
    heads, head_dim, nstate = state_in.shape
    inner = heads * head_dim
    seq_count = lax.axis_size("seq")
    first = lax.axis_index("seq") == 0
    w_x = w_xz[:, 0, :]
    w_z = w_xz[:, 1, :]
    w_out_t = jnp.transpose(w_out)
    widths = (w_x.shape[1], w_z.shape[1], w_bc.shape[1], w_out_t.shape[1])
    packed = jnp.concatenate([w_x, w_z, w_bc, w_out_t], axis=1)
    gathered = lax.all_gather(packed, "seq", axis=0, tiled=True)
    proj = widths[0] + widths[1] + widths[2]
    xzbc = jnp.dot(tokens, gathered[:, :proj], preferred_element_type=jnp.float32)
    w_out_cols = gathered[:, proj:]
    xz = xzbc[:, : 2 * inner]
    bc_sum = xzbc[:, 2 * inner :]
    x_pre = xz[:, :inner].astype(jnp.bfloat16)
    z_val = xz[:, inner:].astype(jnp.bfloat16)
    bc_pre = bc_sum.astype(jnp.bfloat16)
    lag = conv_x.shape[0] - 1
    before_x, before_bc = passed_along((x_pre[rows - lag :], bc_pre[rows - lag :]), "seq", 1)
    before_x = jnp.where(first, tail_x, before_x)
    before_bc = jnp.where(first, tail_bc, before_bc)
    x_conv = depthwise(x_pre, before_x, conv_x)
    bc_conv = depthwise(bc_pre, before_bc, conv_bc)
    b_val = bc_conv[:, :nstate]
    c_val = bc_conv[:, nstate:]
    logdec = -decay_code.astype(jnp.float32) / (16.0 * rows * seq_count)
    blocks = rows // Q
    xb = x_conv.reshape(blocks, Q, heads, head_dim)
    bb = b_val.reshape(blocks, Q, nstate)
    cb = c_val.reshape(blocks, Q, nstate)
    cum = jnp.cumsum(logdec.reshape(blocks, Q, heads), axis=1)
    tail_decay = jnp.exp(cum[:, -1:, :] - cum)
    decayed_b = (
        jnp.transpose(tail_decay, (0, 2, 1))[..., None] * bb.astype(jnp.float32)[:, None]
    ).astype(jnp.bfloat16)
    added = jnp.einsum("bhsn,bshp->bhpn", decayed_b, xb, preferred_element_type=jnp.float32)
    block_decay = jnp.exp(cum[:, -1, :])
    before = [None]
    running = added[0]
    for b in range(1, blocks):
        before.append(running)
        running = block_decay[b][:, None, None] * running + added[b]
    cum_range = jnp.cumsum(logdec, axis=0)
    range_decay = jnp.exp(cum_range[-1])
    incoming = entering_state(range_decay, running, state_in)
    places = jnp.arange(Q)
    lower = places[:, None] >= places[None, :]
    cumt = jnp.transpose(cum, (0, 2, 1))
    diff = cumt[:, :, :, None] - cumt[:, :, None, :]
    decay = jnp.where(lower, jnp.exp(jnp.where(lower, diff, 0.0)), 0.0)
    scores = jnp.einsum("btn,bsn->bts", cb, bb, preferred_element_type=jnp.float32)
    weights = (decay * scores[:, None]).astype(jnp.bfloat16)
    parts = jnp.einsum("bhts,bshp->bthp", weights, xb, preferred_element_type=jnp.float32)
    pieces_out = [parts[0]]
    for b in range(1, blocks):
        carried = jnp.einsum(
            "tn,hpn->thp", cb[b].astype(jnp.float32), before[b], precision=lax.Precision.HIGHEST
        )
        pieces_out.append(parts[b] + carried * jnp.exp(cum[b])[:, :, None])
    parts = jnp.concatenate(pieces_out, axis=0)
    correction = jnp.einsum(
        "tn,hpn->thp", c_val.astype(jnp.float32), incoming, precision=lax.Precision.HIGHEST
    )
    parts = (parts + correction * jnp.exp(cum_range)[:, :, None]).reshape(rows, inner)
    y_val = parts / nstate + jnp.repeat(skip_gain, head_dim)[None, :] * x_conv.astype(jnp.float32)
    gated = y_val * jax.nn.silu(z_val.astype(jnp.float32))
    total_sq = lax.psum(jnp.sum(gated * gated, axis=1), "head")
    meansq = total_sq / (inner * lax.axis_size("head"))
    normed = (gated * lax.rsqrt(meansq[:, None] + 1e-05) * norm_gain[None, :]).astype(jnp.bfloat16)
    partial_out = lax.dot_general(
        normed, w_out_cols, (((1,), (1,)), ((), ())), preferred_element_type=jnp.float32
    )
    result = lax.psum_scatter(partial_out, "head", scatter_dimension=1, tiled=True)
    return result.astype(jnp.bfloat16)


def solution(mesh):
    return jax.shard_map(
        local,
        mesh=mesh,
        in_specs=(
            P("seq", None),
            P("seq", None, "head"),
            P("seq", None),
            P(None, "head"),
            P(),
            P(None, "head"),
            P(),
            P("seq", "head"),
            P("head"),
            P("head", None, None),
            P("head"),
            P("head", "seq"),
        ),
        out_specs=P("seq", "head"),
        check_vma=False,
    )
```

profile of v0, /device:TPU:1, one launch (start us, length us, event | category | flops | bytes accessed | tf_op | source)
XLA Modules:
  0.0 339.5 jit_solution(3522186953847482299)
XLA Ops:
  6.5 0.9 copy.33
  7.5 1.5 fusion.52
  9.4 1.7 pad_maximum_fusion
  11.9 1.1 reduce-window.16
  13.0 1.1 reduce-window.14
  18.4 133.0 %all-gather.2.cloned.1.call-done = bf16[4096,1792]{0,1:T(8,128)(2,1)} async-done(((bf16[128,1792]{0,1:T(8,128)(2,1)}), bf16[4096,1792]{0,1:T(8,128)(2,1)}) %all-gather.2.cloned.1.call-update) | async-done | bytes 14680080 | tf_op jit(solution)/shard_map/all_gather | solution.py:72
  151.4 10.5 %fusion.7 = bf16[512,1280]{1,0:T(8,128)(2,1)S(1)} fusion(bf16[512,4096]{1,0:T(8,128)(2,1)} %param.12, bf16[4096,1792]{0,1:T(8,128)(2,1)} %all-gather.2.cloned.1.call-done), kind=kOutput, calls=%fused_computation.6 | convolution fusion | flops 5369364480 | bytes 15990784 | tf_op jit(solution)/shard_map/dot_general | solution.py:74
  161.9 2.5 collective-permute-start.1
  165.2 3.5 %collective-permute-start = (bf16[3,512]{1,0:T(4,128)(2,1)S(1)}, bf16[3,512]{1,0:T(4,128)(2,1)S(1)}, u32[]{:S(2)}, u32[]{:S(2)}) collective-permute-start(bf16[3,512]{1,0:T(4,128)(2,1)S(1)} %slice.216), channel_id=1, source_target_pairs={{0,8},{8,16},{16,24},{24,32},{32,40},{40,48},{48,56},{56,64},{64,7... | collective-permute-start | bytes 9224 | tf_op jit(solution)/shard_map/ppermute | solution.py:12
  172.5 2.0 fusion.24
  175.9 2.6 collective-permute-start.2
  178.5 3.6 %collective-permute-done.2 = f32[8,65,128]{2,1,0:T(8,128)S(1)} collective-permute-done((f32[8,65,128]{2,1,0:T(8,128)S(1)}, f32[8,65,128]{2,1,0:T(8,128)S(1)}, u32[]{:S(2)}, u32[]{:S(2)}) %collective-permute-start.2) | collective-permute-done | bytes 266272 | tf_op jit(solution)/shard_map/ppermute | solution.py:12
  182.2 1.0 slice_select_fusion
  183.3 4.0 %collective-permute-start.3 = (f32[8,65,128]{2,1,0:T(8,128)S(1)}, f32[8,65,128]{2,1,0:T(8,128)}, u32[]{:S(2)}, u32[]{:S(2)}) collective-permute-start(f32[8,65,128]{2,1,0:T(8,128)S(1)} %pad_maximum_fusion.2), channel_id=1, source_target_pairs={{0,8},{8,16},{16,24},{24,32},{32,40},{40,48},{48,56},{56,64},{64,7... | collective-permute-start | bytes 798728 | tf_op jit(solution)/shard_map/ppermute | solution.py:12
  187.4 2.9 collective-permute-done.3
  191.2 1.1 add_select_fusion.4
  192.4 4.9 %collective-permute-start.4 = (f32[8,65,128]{2,1,0:T(8,128)S(1)}, f32[8,65,128]{2,1,0:T(8,128)}, u32[]{:S(2)}, u32[]{:S(2)}) collective-permute-start(f32[8,65,128]{2,1,0:T(8,128)S(1)} %pad_maximum_fusion.3), channel_id=1, source_target_pairs={{0,16},{8,24},{16,32},{24,40},{32,48},{40,56},{48,64},{56,72},{64,... | collective-permute-start | bytes 798728 | tf_op jit(solution)/shard_map/ppermute | solution.py:12
  198.0 2.3 collective-permute-done.4
  201.2 1.1 add_select_fusion.3
  202.4 13.9 %collective-permute-start.5 = (f32[8,65,128]{2,1,0:T(8,128)S(1)}, f32[8,65,128]{2,1,0:T(8,128)}, u32[]{:S(2)}, u32[]{:S(2)}) collective-permute-start(f32[8,65,128]{2,1,0:T(8,128)S(1)} %pad_maximum_fusion.4), channel_id=1, source_target_pairs={{0,32},{8,40},{16,48},{24,56},{32,64},{40,72},{48,80},{56,88},{64,... | collective-permute-start | bytes 798728 | tf_op jit(solution)/shard_map/ppermute | solution.py:12
  216.7 5.7 %collective-permute-done.5 = f32[8,65,128]{2,1,0:T(8,128)} collective-permute-done((f32[8,65,128]{2,1,0:T(8,128)S(1)}, f32[8,65,128]{2,1,0:T(8,128)}, u32[]{:S(2)}, u32[]{:S(2)}) %collective-permute-start.5) | collective-permute-done | bytes 266272 | tf_op jit(solution)/shard_map/ppermute | solution.py:12
  222.4 1.1 add_select_fusion.2
  224.5 5.7 %collective-permute-start.6 = (f32[8,65,128]{2,1,0:T(8,128)S(1)}, f32[8,65,128]{2,1,0:T(8,128)S(1)}, u32[]{:S(2)}, u32[]{:S(2)}) collective-permute-start(f32[8,65,128]{2,1,0:T(8,128)S(1)} %pad_maximum_fusion.5), channel_id=1, source_target_pairs={{0,64},{8,72},{16,80},{24,88},{32,96},{40,104},{48,112},{56,120},{... | collective-permute-start | bytes 798728 | tf_op jit(solution)/shard_map/ppermute | solution.py:12
  230.2 1.3 fusion.16
  231.5 4.3 %collective-permute-done.6 = f32[8,65,128]{2,1,0:T(8,128)S(1)} collective-permute-done((f32[8,65,128]{2,1,0:T(8,128)S(1)}, f32[8,65,128]{2,1,0:T(8,128)S(1)}, u32[]{:S(2)}, u32[]{:S(2)}) %collective-permute-start.6) | collective-permute-done | bytes 266272 | tf_op jit(solution)/shard_map/ppermute | solution.py:12
  236.1 5.2 %collective-permute-start.7 = (f32[8,65,128]{2,1,0:T(8,128)S(1)}, f32[8,65,128]{2,1,0:T(8,128)S(1)}, u32[]{:S(2)}, u32[]{:S(2)}) collective-permute-start(f32[8,65,128]{2,1,0:T(8,128)S(1)} %pad_maximum_fusion.6), channel_id=1, source_target_pairs={{0,128},{8,136},{16,144},{24,152},{32,160},{40,168},{48,176},{56,1... | collective-permute-start | bytes 798728 | tf_op jit(solution)/shard_map/ppermute | solution.py:12
  241.8 5.8 %collective-permute-done.7 = f32[8,65,128]{2,1,0:T(8,128)S(1)} collective-permute-done((f32[8,65,128]{2,1,0:T(8,128)S(1)}, f32[8,65,128]{2,1,0:T(8,128)S(1)}, u32[]{:S(2)}, u32[]{:S(2)}) %collective-permute-start.7) | collective-permute-done | bytes 266272 | tf_op jit(solution)/shard_map/ppermute | solution.py:12
  248.7 2.1 multiply_reduce_fusion
  250.8 19.7 %psum.7 = f32[512]{0:T(512)S(1)} all-reduce(f32[512]{0:T(512)S(1)} %get-tuple-element.7), channel_id=1, replica_groups=mesh['seq'=32,'head'=8] {'head'}, use_global_device_ids=true, to_apply=%region_5.6 | all-reduce | flops 512 | bytes 4096 | tf_op jit(solution)/shard_map/psum | solution.py:130
  270.5 7.9 %fusion.2 = f32[512,4096]{1,0:T(8,128)} fusion(bf16[4096,1792]{0,1:T(8,128)(2,1)} %all-gather.2.cloned.1.call-done, f32[512,512]{1,0:T(8,128)S(1)} %get-tuple-element.8, f32[512]{0:T(512)S(1)} %copy-done.5, f32[512]{0:T(512)S(1)} %add_rsqrt_fusion), kind=kOutput, calls=%fused_computation.2 | convolution fusion | flops 2148270080 | bytes 13635584 | tf_op jit(solution)/shard_map/dot_general | solution.py:133
  278.4 52.1 %reduce-scatter.2.cloned.1.call-done = f32[512,512]{1,0:T(8,128)} async-done(((f32[512,4096]{1,0:T(8,128)}), f32[512,512]{1,0:T(8,128)}) %reduce-scatter.2.cloned.1.call-update) | async-done | bytes 1048592 | tf_op jit(solution)/shard_map/reduce_scatter | solution.py:136
  330.5 2.1 convert_element_type.56
  (105 shorter events, 17.4 us)
Async XLA Ops:
  6.5 144.9 %all-gather.2.cloned.1.call-start = ((), (), s32[]{:S(2)}) async-start(), calls=%async_computation.1 | async-start | bytes 15138816 | tf_op jit(solution)/shard_map/all_gather | solution.py:72
  11.1 319.5 %reduce-scatter.2.cloned.1.call-start = ((), (), s32[]{:S(2)}) async-start(), calls=%async_computation.2 | async-start | bytes 9437184 | tf_op jit(solution)/shard_map/reduce_scatter | solution.py:136
  14.6 3.1 copy-start.4
  17.0 153.7 %copy-start.6 = (f32[1,512]{1,0:T(1,128)}, f32[1,512]{1,0:T(1,128)S(1)}, u32[]{:S(2)}) copy-start(f32[1,512]{1,0:T(1,128)S(1)} %get-tuple-element.32) | copy-start | bytes 6148
  17.0 153.7 %copy-start.8 = (f32[1,512]{1,0:T(1,128)}, f32[1,512]{1,0:T(1,128)S(1)}, u32[]{:S(2)}) copy-start(f32[1,512]{1,0:T(1,128)S(1)} %get-tuple-element.33) | copy-start | bytes 6148
  17.0 153.7 %copy-start.10 = (f32[1,512]{1,0:T(1,128)}, f32[1,512]{1,0:T(1,128)S(1)}, u32[]{:S(2)}) copy-start(f32[1,512]{1,0:T(1,128)S(1)} %get-tuple-element.34) | copy-start | bytes 6148
  17.0 153.7 %copy-start.12 = (f32[1,512]{1,0:T(1,128)}, f32[1,512]{1,0:T(1,128)S(1)}, u32[]{:S(2)}) copy-start(f32[1,512]{1,0:T(1,128)S(1)} %get-tuple-element.35) | copy-start | bytes 6148
  18.4 150.3 %copy-start.16 = (bf16[3,256]{1,0:T(4,128)(2,1)S(1)}, bf16[3,256]{1,0:T(4,128)(2,1)}, u32[]{:S(2)}) copy-start(bf16[3,256]{1,0:T(4,128)(2,1)} %param.18) | copy-start | bytes 4612
  161.9 6.9 %copy-start = (bf16[512,1280]{1,0:T(8,128)(2,1)}, bf16[512,1280]{1,0:T(8,128)(2,1)S(1)}, u32[]{:S(2)}) copy-start(bf16[512,1280]{1,0:T(8,128)(2,1)S(1)} %fusion.7) | copy-start | bytes 3932164
  161.9 8.6 %copy-start.15 = (bf16[3,512]{1,0:T(4,128)(2,1)S(1)}, bf16[3,512]{1,0:T(4,128)(2,1)}, u32[]{:S(2)}) copy-start(bf16[3,512]{1,0:T(4,128)(2,1)} %param.17) | copy-start | bytes 9220
  161.9 6.8 %collective-permute-start.1 = (bf16[3,256]{1,0:T(4,128)(2,1)S(1)}, bf16[3,256]{1,0:T(4,128)(2,1)S(1)}, u32[]{:S(2)}, u32[]{:S(2)}) collective-permute-start(bf16[3,256]{1,0:T(4,128)(2,1)S(1)} %slice.224), channel_id=1, source_target_pairs={{0,8},{8,16},{16,24},{24,32},{32,40},{40,48},{48,56},{56,64},{64,7... | collective-permute-start | bytes 4616 | tf_op jit(solution)/shard_map/ppermute | solution.py:12
  165.2 5.3 %collective-permute-start = (bf16[3,512]{1,0:T(4,128)(2,1)S(1)}, bf16[3,512]{1,0:T(4,128)(2,1)S(1)}, u32[]{:S(2)}, u32[]{:S(2)}) collective-permute-start(bf16[3,512]{1,0:T(4,128)(2,1)S(1)} %slice.216), channel_id=1, source_target_pairs={{0,8},{8,16},{16,24},{24,32},{32,40},{40,48},{48,56},{56,64},{64,7... | collective-permute-start | bytes 9224 | tf_op jit(solution)/shard_map/ppermute | solution.py:12
  172.5 43.8 %copy-start.17 = (f32[8]{0:T(128)S(1)}, f32[8]{0:T(128)}, u32[]{:S(2)}) copy-start(f32[8]{0:T(128)} %param.20) | copy-start | bytes 100
  172.5 44.0 %copy-start.1 = (bf16[512,128]{1,0:T(8,128)(2,1)S(1)}, bf16[512,128]{1,0:T(8,128)(2,1)}, u32[]{:S(2)}) copy-start(bf16[512,128]{1,0:T(8,128)(2,1)} %get-tuple-element.27) | copy-start | bytes 393220
  174.5 55.7 %copy-start.14 = (f32[2,8,256]{2,1,0:T(8,128)S(1)}, f32[2,8,256]{2,1,0:T(8,128)}, u32[]{:S(2)}) copy-start(f32[2,8,256]{2,1,0:T(8,128)} %get-tuple-element.22) | copy-start | bytes 49156
  175.9 6.2 %collective-permute-start.2 = (f32[8,65,128]{2,1,0:T(8,128)S(1)}, f32[8,65,128]{2,1,0:T(8,128)S(1)}, u32[]{:S(2)}, u32[]{:S(2)}) collective-permute-start(f32[8,65,128]{2,1,0:T(8,128)S(1)} %pad_maximum_fusion.1), channel_id=1, source_target_pairs={{0,8},{8,16},{16,24},{24,32},{32,40},{40,48},{48,56},{56,64},{64,7... | collective-permute-start | bytes 798728 | tf_op jit(solution)/shard_map/ppermute | solution.py:12
  182.1 1.2 copy-start.2
  183.3 7.0 %collective-permute-start.3 = (f32[8,65,128]{2,1,0:T(8,128)S(1)}, f32[8,65,128]{2,1,0:T(8,128)}, u32[]{:S(2)}, u32[]{:S(2)}) collective-permute-start(f32[8,65,128]{2,1,0:T(8,128)S(1)} %pad_maximum_fusion.2), channel_id=1, source_target_pairs={{0,8},{8,16},{16,24},{24,32},{32,40},{40,48},{48,56},{56,64},{64,7... | collective-permute-start | bytes 798728 | tf_op jit(solution)/shard_map/ppermute | solution.py:12
  192.4 7.9 %collective-permute-start.4 = (f32[8,65,128]{2,1,0:T(8,128)S(1)}, f32[8,65,128]{2,1,0:T(8,128)}, u32[]{:S(2)}, u32[]{:S(2)}) collective-permute-start(f32[8,65,128]{2,1,0:T(8,128)S(1)} %pad_maximum_fusion.3), channel_id=1, source_target_pairs={{0,16},{8,24},{16,32},{24,40},{32,48},{40,56},{48,64},{56,72},{64,... | collective-permute-start | bytes 798728 | tf_op jit(solution)/shard_map/ppermute | solution.py:12
  202.4 20.0 %collective-permute-start.5 = (f32[8,65,128]{2,1,0:T(8,128)S(1)}, f32[8,65,128]{2,1,0:T(8,128)}, u32[]{:S(2)}, u32[]{:S(2)}) collective-permute-start(f32[8,65,128]{2,1,0:T(8,128)S(1)} %pad_maximum_fusion.4), channel_id=1, source_target_pairs={{0,32},{8,40},{16,48},{24,56},{32,64},{40,72},{48,80},{56,88},{64,... | collective-permute-start | bytes 798728 | tf_op jit(solution)/shard_map/ppermute | solution.py:12
  224.5 11.3 %collective-permute-start.6 = (f32[8,65,128]{2,1,0:T(8,128)S(1)}, f32[8,65,128]{2,1,0:T(8,128)S(1)}, u32[]{:S(2)}, u32[]{:S(2)}) collective-permute-start(f32[8,65,128]{2,1,0:T(8,128)S(1)} %pad_maximum_fusion.5), channel_id=1, source_target_pairs={{0,64},{8,72},{16,80},{24,88},{32,96},{40,104},{48,112},{56,120},{... | collective-permute-start | bytes 798728 | tf_op jit(solution)/shard_map/ppermute | solution.py:12
  230.2 17.4 %copy-start.3 = (f32[512,8]{0,1:T(8,128)S(1)}, f32[512,8]{0,1:T(8,128)}, u32[]{:S(2)}) copy-start(f32[512,8]{0,1:T(8,128)} %get-tuple-element.19) | copy-start | bytes 49156
  235.9 12.8 %copy-start.7 = (f32[1,512]{1,0:T(1,128)S(1)}, f32[1,512]{1,0:T(1,128)}, u32[]{:S(2)}) copy-start(f32[1,512]{1,0:T(1,128)} %copy-done.6) | copy-start | bytes 6148
  235.9 12.8 %copy-start.9 = (f32[1,512]{1,0:T(1,128)S(1)}, f32[1,512]{1,0:T(1,128)}, u32[]{:S(2)}) copy-start(f32[1,512]{1,0:T(1,128)} %copy-done.8) | copy-start | bytes 6148
  235.9 12.8 %copy-start.11 = (f32[1,512]{1,0:T(1,128)S(1)}, f32[1,512]{1,0:T(1,128)}, u32[]{:S(2)}) copy-start(f32[1,512]{1,0:T(1,128)} %copy-done.10) | copy-start | bytes 6148
  235.9 12.8 %copy-start.13 = (f32[1,512]{1,0:T(1,128)S(1)}, f32[1,512]{1,0:T(1,128)}, u32[]{:S(2)}) copy-start(f32[1,512]{1,0:T(1,128)} %copy-done.12) | copy-start | bytes 6148
  236.1 11.5 %collective-permute-start.7 = (f32[8,65,128]{2,1,0:T(8,128)S(1)}, f32[8,65,128]{2,1,0:T(8,128)S(1)}, u32[]{:S(2)}, u32[]{:S(2)}) collective-permute-start(f32[8,65,128]{2,1,0:T(8,128)S(1)} %pad_maximum_fusion.6), channel_id=1, source_target_pairs={{0,128},{8,136},{16,144},{24,152},{32,160},{40,168},{48,176},{56,1... | collective-permute-start | bytes 798728 | tf_op jit(solution)/shard_map/ppermute | solution.py:12
  248.3 22.2 %copy-start.5 = (f32[512]{0:T(512)S(1)}, f32[512]{0:T(512)}, u32[]{:S(2)}) copy-start(f32[512]{0:T(512)} %param.22) | copy-start | bytes 6148
Sparse Core Ops, SparseCore 0:
  11.2 140.1 all-gather.1
  278.5 51.9 reduce-scatter.1
where the time goes:
time: 341 us; the launch traced here: 339 us
  waiting for transfers between devices  210 us (62%)
  starting transfers between devices  42.4 us (12%)
  matrix products  22.9 us (7%)
  other arithmetic  20.5 us (6%)
  blocking collectives  19.7 us (6%)
  between operations  13.9 us (4%)
  local copies, waits for them, and re-layouts  10.3 us (3%)
    all_gather x1, waiting for transfers between devices, local(): gathered = lax.all_gather(packed, 'seq', axis=0, tiled=True)  133 us
    reduce_scatter x1, waiting for transfers between devices, local(): lax.psum_scatter(partial_out, 'head', scatter_dimension=1, tiled=True)  52.1 us
    ppermute x8, starting transfers between devices, passed_along(): return lax.ppermute(value, axis, pairs)  42.4 us
    ppermute x8, waiting for transfers between devices, passed_along(): return lax.ppermute(value, axis, pairs)  24.6 us
    psum x1, blocking collectives, local(): total_sq = lax.psum(jnp.sum(gated * gated, axis=1), 'head')  19.7 us
    dot_general x1, matrix products, local(): jnp.dot(tokens, gathered[:, :proj], preferred_element_type=jnp.float32)  10.5 us
    dot_general x1, matrix products, local(): lax.dot_general(normed, w_out_cols, (((1,), (1,)), ((), ())), preferred_e...  7.87 us
  transfers between devices with their start and end apart: 10, of which 8 were waited for; matrix products, arithmetic and copies ran while one was open for 4% of the time, Pallas kernels for 0%

commit v1 on v0

--- a/solution.py
+++ b/solution.py
@@ -127,7 +127,7 @@
     parts = (parts + correction * jnp.exp(cum_range)[:, :, None]).reshape(rows, inner)
     y_val = parts / nstate + jnp.repeat(skip_gain, head_dim)[None, :] * x_conv.astype(jnp.float32)
     gated = y_val * jax.nn.silu(z_val.astype(jnp.float32))
-    total_sq = lax.psum(jnp.sum(gated * gated, axis=1), "head")
+    total_sq = jnp.sum(lax.all_gather(jnp.sum(gated * gated, axis=1), "head"), axis=0)
     meansq = total_sq / (inner * lax.axis_size("head"))
     normed = (gated * lax.rsqrt(meansq[:, None] + 1e-05) * norm_gain[None, :]).astype(jnp.bfloat16)
     partial_out = lax.dot_general(

time: 341 us -> 341 us (level)
    psum x1 -> x0, blocking collectives: 19.7 us -> none  [local(): total_sq = lax.psum(jnp.sum(gated * gated, axis=1), 'head')]
    all_gather x0 -> x1, blocking collectives: none -> 19.6 us  [local(): lax.all_gather(jnp.sum(gated * gated, axis=1), 'head')]
where the time goes in v1:
time: 341 us; the launch traced here: 340 us
  waiting for transfers between devices  211 us (62%)
  starting transfers between devices  42.4 us (12%)
  matrix products  22.9 us (7%)
  other arithmetic  20.5 us (6%)
  blocking collectives  19.6 us (6%)
  between operations  13.9 us (4%)
  local copies, waits for them, and re-layouts  10.3 us (3%)
    all_gather x1, waiting for transfers between devices, local(): gathered = lax.all_gather(packed, 'seq', axis=0, tiled=True)  133 us
    reduce_scatter x1, waiting for transfers between devices, local(): lax.psum_scatter(partial_out, 'head', scatter_dimension=1, tiled=True)  52.9 us
    ppermute x8, starting transfers between devices, passed_along(): return lax.ppermute(value, axis, pairs)  42.4 us
    ppermute x8, waiting for transfers between devices, passed_along(): return lax.ppermute(value, axis, pairs)  24.6 us
    all_gather x1, blocking collectives, local(): lax.all_gather(jnp.sum(gated * gated, axis=1), 'head')  19.6 us
    dot_general x1, matrix products, local(): jnp.dot(tokens, gathered[:, :proj], preferred_element_type=jnp.float32)  10.5 us
    dot_general x1, matrix products, local(): lax.dot_general(normed, w_out_cols, (((1,), (1,)), ((), ())), preferred_e...  7.87 us
  transfers between devices with their start and end apart: 10, of which 8 were waited for; matrix products, arithmetic and copies ran while one was open for 4% of the time, Pallas kernels for 0%

profile of v1, /device:TPU:1, one launch (start us, length us, event | category | flops | bytes accessed | tf_op | source)
XLA Modules:
  0.0 340.2 jit_solution(9110661409957370922)
XLA Ops:
  6.5 0.9 copy.40
  7.5 1.5 fusion.52
  9.4 1.7 pad_maximum_fusion
  11.9 1.1 reduce-window.16
  13.0 1.1 reduce-window.14
  18.4 133.0 %all-gather.4.cloned.1.call-done = bf16[4096,1792]{0,1:T(8,128)(2,1)} async-done(((bf16[128,1792]{0,1:T(8,128)(2,1)}), bf16[4096,1792]{0,1:T(8,128)(2,1)}) %all-gather.4.cloned.1.call-update) | async-done | bytes 14680080 | tf_op jit(solution)/shard_map/all_gather | solution.py:72
  151.4 10.5 %fusion.7 = bf16[512,1280]{1,0:T(8,128)(2,1)S(1)} fusion(bf16[512,4096]{1,0:T(8,128)(2,1)} %param.12, bf16[4096,1792]{0,1:T(8,128)(2,1)} %all-gather.4.cloned.1.call-done), kind=kOutput, calls=%fused_computation.6 | convolution fusion | flops 5369364480 | bytes 15990784 | tf_op jit(solution)/shard_map/dot_general | solution.py:74
  161.9 2.5 collective-permute-start.1
  165.2 3.5 %collective-permute-start = (bf16[3,512]{1,0:T(4,128)(2,1)S(1)}, bf16[3,512]{1,0:T(4,128)(2,1)S(1)}, u32[]{:S(2)}, u32[]{:S(2)}) collective-permute-start(bf16[3,512]{1,0:T(4,128)(2,1)S(1)} %slice.216), channel_id=1, source_target_pairs={{0,8},{8,16},{16,24},{24,32},{32,40},{40,48},{48,56},{56,64},{64,7... | collective-permute-start | bytes 9224 | tf_op jit(solution)/shard_map/ppermute | solution.py:12
  172.5 2.0 fusion.24
  175.9 2.6 collective-permute-start.2
  178.5 3.6 %collective-permute-done.2 = f32[8,65,128]{2,1,0:T(8,128)S(1)} collective-permute-done((f32[8,65,128]{2,1,0:T(8,128)S(1)}, f32[8,65,128]{2,1,0:T(8,128)S(1)}, u32[]{:S(2)}, u32[]{:S(2)}) %collective-permute-start.2) | collective-permute-done | bytes 266272 | tf_op jit(solution)/shard_map/ppermute | solution.py:12
  182.2 1.0 slice_select_fusion
  183.3 4.0 %collective-permute-start.3 = (f32[8,65,128]{2,1,0:T(8,128)S(1)}, f32[8,65,128]{2,1,0:T(8,128)}, u32[]{:S(2)}, u32[]{:S(2)}) collective-permute-start(f32[8,65,128]{2,1,0:T(8,128)S(1)} %pad_maximum_fusion.2), channel_id=1, source_target_pairs={{0,8},{8,16},{16,24},{24,32},{32,40},{40,48},{48,56},{56,64},{64,7... | collective-permute-start | bytes 798728 | tf_op jit(solution)/shard_map/ppermute | solution.py:12
  187.4 2.9 collective-permute-done.3
  191.2 1.1 add_select_fusion.4
  192.4 4.9 %collective-permute-start.4 = (f32[8,65,128]{2,1,0:T(8,128)S(1)}, f32[8,65,128]{2,1,0:T(8,128)}, u32[]{:S(2)}, u32[]{:S(2)}) collective-permute-start(f32[8,65,128]{2,1,0:T(8,128)S(1)} %pad_maximum_fusion.3), channel_id=1, source_target_pairs={{0,16},{8,24},{16,32},{24,40},{32,48},{40,56},{48,64},{56,72},{64,... | collective-permute-start | bytes 798728 | tf_op jit(solution)/shard_map/ppermute | solution.py:12
  198.0 2.3 collective-permute-done.4
  201.2 1.1 add_select_fusion.3
  202.4 13.9 %collective-permute-start.5 = (f32[8,65,128]{2,1,0:T(8,128)S(1)}, f32[8,65,128]{2,1,0:T(8,128)}, u32[]{:S(2)}, u32[]{:S(2)}) collective-permute-start(f32[8,65,128]{2,1,0:T(8,128)S(1)} %pad_maximum_fusion.4), channel_id=1, source_target_pairs={{0,32},{8,40},{16,48},{24,56},{32,64},{40,72},{48,80},{56,88},{64,... | collective-permute-start | bytes 798728 | tf_op jit(solution)/shard_map/ppermute | solution.py:12
  216.7 5.7 %collective-permute-done.5 = f32[8,65,128]{2,1,0:T(8,128)} collective-permute-done((f32[8,65,128]{2,1,0:T(8,128)S(1)}, f32[8,65,128]{2,1,0:T(8,128)}, u32[]{:S(2)}, u32[]{:S(2)}) %collective-permute-start.5) | collective-permute-done | bytes 266272 | tf_op jit(solution)/shard_map/ppermute | solution.py:12
  222.4 1.1 add_select_fusion.2
  224.5 5.7 %collective-permute-start.6 = (f32[8,65,128]{2,1,0:T(8,128)S(1)}, f32[8,65,128]{2,1,0:T(8,128)S(1)}, u32[]{:S(2)}, u32[]{:S(2)}) collective-permute-start(f32[8,65,128]{2,1,0:T(8,128)S(1)} %pad_maximum_fusion.5), channel_id=1, source_target_pairs={{0,64},{8,72},{16,80},{24,88},{32,96},{40,104},{48,112},{56,120},{... | collective-permute-start | bytes 798728 | tf_op jit(solution)/shard_map/ppermute | solution.py:12
  230.2 1.3 fusion.16
  231.5 4.3 %collective-permute-done.6 = f32[8,65,128]{2,1,0:T(8,128)S(1)} collective-permute-done((f32[8,65,128]{2,1,0:T(8,128)S(1)}, f32[8,65,128]{2,1,0:T(8,128)S(1)}, u32[]{:S(2)}, u32[]{:S(2)}) %collective-permute-start.6) | collective-permute-done | bytes 266272 | tf_op jit(solution)/shard_map/ppermute | solution.py:12
  236.1 5.2 %collective-permute-start.7 = (f32[8,65,128]{2,1,0:T(8,128)S(1)}, f32[8,65,128]{2,1,0:T(8,128)S(1)}, u32[]{:S(2)}, u32[]{:S(2)}) collective-permute-start(f32[8,65,128]{2,1,0:T(8,128)S(1)} %pad_maximum_fusion.6), channel_id=1, source_target_pairs={{0,128},{8,136},{16,144},{24,152},{32,160},{40,168},{48,176},{56,1... | collective-permute-start | bytes 798728 | tf_op jit(solution)/shard_map/ppermute | solution.py:12
  241.8 5.8 %collective-permute-done.7 = f32[8,65,128]{2,1,0:T(8,128)S(1)} collective-permute-done((f32[8,65,128]{2,1,0:T(8,128)S(1)}, f32[8,65,128]{2,1,0:T(8,128)S(1)}, u32[]{:S(2)}, u32[]{:S(2)}) %collective-permute-start.7) | collective-permute-done | bytes 266272 | tf_op jit(solution)/shard_map/ppermute | solution.py:12
  248.7 2.1 multiply_reduce_fusion
  250.8 19.6 %all-gather.1 = f32[8,1,512]{2,1,0:T(1,128)S(1)} all-gather(f32[1,1,512]{2,1,0:T(1,128)S(1)} %bitcast.85), channel_id=2, replica_groups=mesh['seq'=32,'head'=8] {'head'}, dimensions={0}, use_global_device_ids=true | all-gather | bytes 18432 | tf_op jit(solution)/shard_map/all_gather | solution.py:130
  270.5 7.9 %fusion.2 = f32[512,4096]{1,0:T(8,128)} fusion(bf16[4096,1792]{0,1:T(8,128)(2,1)} %all-gather.4.cloned.1.call-done, f32[512,512]{1,0:T(8,128)S(1)} %get-tuple-element.8, f32[512]{0:T(512)S(1)} %copy-done.5, f32[512]{0:T(512)S(1)} %add_rsqrt_fusion), kind=kOutput, calls=%fused_computation.2 | convolution fusion | flops 2148270080 | bytes 13635584 | tf_op jit(solution)/shard_map/dot_general | solution.py:133
  278.4 52.9 %reduce-scatter.2.cloned.1.call-done = f32[512,512]{1,0:T(8,128)} async-done(((f32[512,4096]{1,0:T(8,128)}), f32[512,512]{1,0:T(8,128)}) %reduce-scatter.2.cloned.1.call-update) | async-done | bytes 1048592 | tf_op jit(solution)/shard_map/reduce_scatter | solution.py:136
  331.3 2.1 convert_element_type.56
  (106 shorter events, 17.4 us)
Async XLA Ops:
  6.5 144.9 %all-gather.4.cloned.1.call-start = ((), (), s32[]{:S(2)}) async-start(), calls=%async_computation.1 | async-start | bytes 15138816 | tf_op jit(solution)/shard_map/all_gather | solution.py:72
  11.1 320.2 %reduce-scatter.2.cloned.1.call-start = ((), (), s32[]{:S(2)}) async-start(), calls=%async_computation.2 | async-start | bytes 9437184 | tf_op jit(solution)/shard_map/reduce_scatter | solution.py:136
  14.6 3.1 copy-start.4
  17.0 153.7 %copy-start.6 = (f32[1,512]{1,0:T(1,128)}, f32[1,512]{1,0:T(1,128)S(1)}, u32[]{:S(2)}) copy-start(f32[1,512]{1,0:T(1,128)S(1)} %get-tuple-element.32) | copy-start | bytes 6148
  17.0 153.7 %copy-start.8 = (f32[1,512]{1,0:T(1,128)}, f32[1,512]{1,0:T(1,128)S(1)}, u32[]{:S(2)}) copy-start(f32[1,512]{1,0:T(1,128)S(1)} %get-tuple-element.33) | copy-start | bytes 6148
  17.0 153.7 %copy-start.10 = (f32[1,512]{1,0:T(1,128)}, f32[1,512]{1,0:T(1,128)S(1)}, u32[]{:S(2)}) copy-start(f32[1,512]{1,0:T(1,128)S(1)} %get-tuple-element.34) | copy-start | bytes 6148
  17.0 153.7 %copy-start.12 = (f32[1,512]{1,0:T(1,128)}, f32[1,512]{1,0:T(1,128)S(1)}, u32[]{:S(2)}) copy-start(f32[1,512]{1,0:T(1,128)S(1)} %get-tuple-element.35) | copy-start | bytes 6148
  18.4 150.3 %copy-start.16 = (bf16[3,256]{1,0:T(4,128)(2,1)S(1)}, bf16[3,256]{1,0:T(4,128)(2,1)}, u32[]{:S(2)}) copy-start(bf16[3,256]{1,0:T(4,128)(2,1)} %param.18) | copy-start | bytes 4612
  161.9 6.9 %copy-start = (bf16[512,1280]{1,0:T(8,128)(2,1)}, bf16[512,1280]{1,0:T(8,128)(2,1)S(1)}, u32[]{:S(2)}) copy-start(bf16[512,1280]{1,0:T(8,128)(2,1)S(1)} %fusion.7) | copy-start | bytes 3932164
  161.9 8.6 %copy-start.15 = (bf16[3,512]{1,0:T(4,128)(2,1)S(1)}, bf16[3,512]{1,0:T(4,128)(2,1)}, u32[]{:S(2)}) copy-start(bf16[3,512]{1,0:T(4,128)(2,1)} %param.17) | copy-start | bytes 9220
  161.9 6.8 %collective-permute-start.1 = (bf16[3,256]{1,0:T(4,128)(2,1)S(1)}, bf16[3,256]{1,0:T(4,128)(2,1)S(1)}, u32[]{:S(2)}, u32[]{:S(2)}) collective-permute-start(bf16[3,256]{1,0:T(4,128)(2,1)S(1)} %slice.224), channel_id=1, source_target_pairs={{0,8},{8,16},{16,24},{24,32},{32,40},{40,48},{48,56},{56,64},{64,7... | collective-permute-start | bytes 4616 | tf_op jit(solution)/shard_map/ppermute | solution.py:12
  165.2 5.3 %collective-permute-start = (bf16[3,512]{1,0:T(4,128)(2,1)S(1)}, bf16[3,512]{1,0:T(4,128)(2,1)S(1)}, u32[]{:S(2)}, u32[]{:S(2)}) collective-permute-start(bf16[3,512]{1,0:T(4,128)(2,1)S(1)} %slice.216), channel_id=1, source_target_pairs={{0,8},{8,16},{16,24},{24,32},{32,40},{40,48},{48,56},{56,64},{64,7... | collective-permute-start | bytes 9224 | tf_op jit(solution)/shard_map/ppermute | solution.py:12
  172.5 43.8 %copy-start.17 = (f32[8]{0:T(128)S(1)}, f32[8]{0:T(128)}, u32[]{:S(2)}) copy-start(f32[8]{0:T(128)} %param.20) | copy-start | bytes 100
  172.5 44.0 %copy-start.1 = (bf16[512,128]{1,0:T(8,128)(2,1)S(1)}, bf16[512,128]{1,0:T(8,128)(2,1)}, u32[]{:S(2)}) copy-start(bf16[512,128]{1,0:T(8,128)(2,1)} %get-tuple-element.27) | copy-start | bytes 393220
  174.5 55.7 %copy-start.14 = (f32[2,8,256]{2,1,0:T(8,128)S(1)}, f32[2,8,256]{2,1,0:T(8,128)}, u32[]{:S(2)}) copy-start(f32[2,8,256]{2,1,0:T(8,128)} %get-tuple-element.22) | copy-start | bytes 49156
  175.9 6.2 %collective-permute-start.2 = (f32[8,65,128]{2,1,0:T(8,128)S(1)}, f32[8,65,128]{2,1,0:T(8,128)S(1)}, u32[]{:S(2)}, u32[]{:S(2)}) collective-permute-start(f32[8,65,128]{2,1,0:T(8,128)S(1)} %pad_maximum_fusion.1), channel_id=1, source_target_pairs={{0,8},{8,16},{16,24},{24,32},{32,40},{40,48},{48,56},{56,64},{64,7... | collective-permute-start | bytes 798728 | tf_op jit(solution)/shard_map/ppermute | solution.py:12
  182.1 1.2 copy-start.2
  183.3 7.0 %collective-permute-start.3 = (f32[8,65,128]{2,1,0:T(8,128)S(1)}, f32[8,65,128]{2,1,0:T(8,128)}, u32[]{:S(2)}, u32[]{:S(2)}) collective-permute-start(f32[8,65,128]{2,1,0:T(8,128)S(1)} %pad_maximum_fusion.2), channel_id=1, source_target_pairs={{0,8},{8,16},{16,24},{24,32},{32,40},{40,48},{48,56},{56,64},{64,7... | collective-permute-start | bytes 798728 | tf_op jit(solution)/shard_map/ppermute | solution.py:12
  192.4 7.9 %collective-permute-start.4 = (f32[8,65,128]{2,1,0:T(8,128)S(1)}, f32[8,65,128]{2,1,0:T(8,128)}, u32[]{:S(2)}, u32[]{:S(2)}) collective-permute-start(f32[8,65,128]{2,1,0:T(8,128)S(1)} %pad_maximum_fusion.3), channel_id=1, source_target_pairs={{0,16},{8,24},{16,32},{24,40},{32,48},{40,56},{48,64},{56,72},{64,... | collective-permute-start | bytes 798728 | tf_op jit(solution)/shard_map/ppermute | solution.py:12
  202.4 20.0 %collective-permute-start.5 = (f32[8,65,128]{2,1,0:T(8,128)S(1)}, f32[8,65,128]{2,1,0:T(8,128)}, u32[]{:S(2)}, u32[]{:S(2)}) collective-permute-start(f32[8,65,128]{2,1,0:T(8,128)S(1)} %pad_maximum_fusion.4), channel_id=1, source_target_pairs={{0,32},{8,40},{16,48},{24,56},{32,64},{40,72},{48,80},{56,88},{64,... | collective-permute-start | bytes 798728 | tf_op jit(solution)/shard_map/ppermute | solution.py:12
  224.5 11.3 %collective-permute-start.6 = (f32[8,65,128]{2,1,0:T(8,128)S(1)}, f32[8,65,128]{2,1,0:T(8,128)S(1)}, u32[]{:S(2)}, u32[]{:S(2)}) collective-permute-start(f32[8,65,128]{2,1,0:T(8,128)S(1)} %pad_maximum_fusion.5), channel_id=1, source_target_pairs={{0,64},{8,72},{16,80},{24,88},{32,96},{40,104},{48,112},{56,120},{... | collective-permute-start | bytes 798728 | tf_op jit(solution)/shard_map/ppermute | solution.py:12
  230.2 17.4 %copy-start.3 = (f32[512,8]{0,1:T(8,128)S(1)}, f32[512,8]{0,1:T(8,128)}, u32[]{:S(2)}) copy-start(f32[512,8]{0,1:T(8,128)} %get-tuple-element.19) | copy-start | bytes 49156
  235.9 12.8 %copy-start.7 = (f32[1,512]{1,0:T(1,128)S(1)}, f32[1,512]{1,0:T(1,128)}, u32[]{:S(2)}) copy-start(f32[1,512]{1,0:T(1,128)} %copy-done.6) | copy-start | bytes 6148
  235.9 12.8 %copy-start.9 = (f32[1,512]{1,0:T(1,128)S(1)}, f32[1,512]{1,0:T(1,128)}, u32[]{:S(2)}) copy-start(f32[1,512]{1,0:T(1,128)} %copy-done.8) | copy-start | bytes 6148
  235.9 12.8 %copy-start.11 = (f32[1,512]{1,0:T(1,128)S(1)}, f32[1,512]{1,0:T(1,128)}, u32[]{:S(2)}) copy-start(f32[1,512]{1,0:T(1,128)} %copy-done.10) | copy-start | bytes 6148
  235.9 12.8 %copy-start.13 = (f32[1,512]{1,0:T(1,128)S(1)}, f32[1,512]{1,0:T(1,128)}, u32[]{:S(2)}) copy-start(f32[1,512]{1,0:T(1,128)} %copy-done.12) | copy-start | bytes 6148
  236.1 11.5 %collective-permute-start.7 = (f32[8,65,128]{2,1,0:T(8,128)S(1)}, f32[8,65,128]{2,1,0:T(8,128)S(1)}, u32[]{:S(2)}, u32[]{:S(2)}) collective-permute-start(f32[8,65,128]{2,1,0:T(8,128)S(1)} %pad_maximum_fusion.6), channel_id=1, source_target_pairs={{0,128},{8,136},{16,144},{24,152},{32,160},{40,168},{48,176},{56,1... | collective-permute-start | bytes 798728 | tf_op jit(solution)/shard_map/ppermute | solution.py:12
  248.3 22.2 %copy-start.5 = (f32[512]{0:T(512)S(1)}, f32[512]{0:T(512)}, u32[]{:S(2)}) copy-start(f32[512]{0:T(512)} %param.22) | copy-start | bytes 6148
Sparse Core Ops, SparseCore 0:
  11.2 140.1 all-gather.3
  278.5 52.7 reduce-scatter.1
